TPU v7x, 512 devices: a whole 4x8x8 slice. The times are simulated.
512 devices in a mesh: vox: 32 (over x, z), smp: 16 (over y, core).
Axes of the slice: x: 4, y: 8, z: 8, core: 2. Of those that a mesh axis runs over, the one named last changes fastest.
Arguments:
- ensemble: float32 [4096, 128, 128], P('vox', 'smp'), may hold values from -6 to 6
- voxel_factor: float32 [4096, 128], P('vox'), may hold values from -6 to 6
- sample_factor: float32 [128, 128], P('smp'), may hold values from -6 to 6
- time_factor: float32 [128, 128], replicated, may hold values from -6 to 6
- weights: float32 [128], replicated, may hold values from 0.005 to 0.02
Outputs:
- voxel_result: float32 [4096, 128], P('vox')
- sample_result: float32 [128, 128], P('smp')
- time_result: float32 [128, 128], replicated
- scale_result: float32 [128], replicated
All inputs are finite; a program needn't handle non-finite values. Where the computation divides by a largest or mean magnitude, that divisor is 1e-20 or more.
Results may differ from a plain program's by a relative error of at most 0.0001.
Values sent between devices are 32-bit elements; how exact they have to be, the bound alone decides.
A program may use at most 64 MiB of HBM per device.

v0:
```python
import jax
import jax.numpy as jnp
from jax import lax
from jax.sharding import PartitionSpec as P

HIGH = lax.Precision.HIGHEST


def descend(factor, terms, hadamard, weights):
    coupled = weights[:, None] * weights[None, :] * hadamard
    step_size = 1.0 / jnp.max(jnp.sum(jnp.abs(coupled), axis=1))
    product = jnp.dot(factor, coupled, precision=HIGH, preferred_element_type=jnp.float32)
    return factor - step_size * (product - terms * weights[None, :])


def rescale(moved, gram, row_count):
    scales = jnp.sqrt(jnp.diagonal(gram) / row_count + 1e-06)
    return (moved / scales[None, :], gram / (scales[:, None] * scales[None, :]), scales)


def local_gram(moved):
    return jnp.dot(moved.T, moved, precision=HIGH, preferred_element_type=jnp.float32)


def per_device(ensemble, voxel_factor, sample_factor, time_factor, weights):
    vox_rows, smp_rows, time_count = ensemble.shape
    rank_count = voxel_factor.shape[1]
    voxel_total = vox_rows * lax.axis_size("vox")
    sample_total = smp_rows * lax.axis_size("smp")
    flat = ensemble.reshape(vox_rows * smp_rows, time_count)
    gram_b = lax.psum(local_gram(sample_factor), "smp")
    gram_c = local_gram(time_factor)
    contracted = jnp.dot(flat, time_factor, precision=HIGH, preferred_element_type=jnp.float32)
    contracted = contracted.reshape(vox_rows, smp_rows, rank_count)
    partial_value = jnp.einsum("ijr,jr->ir", contracted, sample_factor, precision=HIGH)
    terms_a = lax.psum(partial_value, "smp")
    moved = descend(voxel_factor, terms_a, gram_b * gram_c, weights)
    gram = lax.psum(local_gram(moved), "vox")
    voxel_factor, gram_a, scales = rescale(moved, gram, voxel_total)
    partial_b = jnp.einsum("ijr,ir->jr", contracted, voxel_factor, precision=HIGH)
    terms_b = lax.psum(partial_b, "vox")
    weights = weights * scales
    moved = descend(sample_factor, terms_b, gram_a * gram_c, weights)
    gram = lax.psum(local_gram(moved), "smp")
    sample_factor, gram_b, scales = rescale(moved, gram, sample_total)
    paired = (voxel_factor[:, None, :] * sample_factor[None, :, :]).reshape(
        vox_rows * smp_rows, rank_count
    )
    partial_c = jnp.einsum("nk,nr->kr", flat, paired, precision=HIGH)
    terms_c = lax.psum(partial_c, ("vox", "smp"))
    weights = weights * scales
    moved = descend(time_factor, terms_c, gram_a * gram_b, weights)
    time_factor, gram_c, scales = rescale(moved, local_gram(moved), time_count)
    weights = weights * scales
    return (voxel_factor, sample_factor, time_factor, weights)


def solution(mesh):
    return jax.shard_map(
        per_device,
        mesh=mesh,
        in_specs=(P("vox", "smp", None), P("vox", None), P("smp", None), P(), P()),
        out_specs=(P("vox", None), P("smp", None), P(), P()),
        check_vma=False,
    )
```

profile of v0, /device:TPU:1, one launch (start us, length us, event | category | flops | bytes accessed | tf_op | source)
XLA Modules:
  0.0 745.5 jit_solution(5589847889184685163)
XLA Ops:
  7.2 0.0 copy-start.3
  7.2 0.0 all-reduce.12.cloned.1.call-start
  7.2 0.0 copy-start.6
  7.2 1.7 fusion.19
  8.9 2.2 multiply_reduce_fusion.1
  11.2 0.0 all-reduce.12.cloned.1.call-update
  11.2 0.0 copy-start.10
  11.2 0.0 all-reduce.6.cloned.1.call-start
  11.3 120.5 %all-reduce.12.cloned.1.call-done = (f32[128,128]{1,0:T(8,128)}, f32[128,128]{1,0:T(8,128)}) async-done(((f32[128,128]{1,0:T(8,128)}, f32[128,128]{1,0:T(8,128)}), (f32[128,128]{1,0:T(8,128)}, f32[128,128]{1,0:T(8,128)})) %all-reduce.12.cloned.1.call-update) | async-done | bytes 131088 | tf_op jit(solution)/shard_map/psum | solution.py:36
  131.8 0.0 copy-done.10
  131.8 1.3 abs_reduce_fusion.2
  133.1 0.6 reduce_max.27
  134.4 0.0 copy-done.5
  134.4 0.0 copy-done.7
  134.4 0.0 copy-done.8
  134.4 0.3 fusion.5
  134.7 0.9 fusion.20
  135.6 0.0 all-reduce.6.cloned.1.call-update
  135.7 0.0 all-reduce.8.cloned.1.call-start
  135.7 149.7 %all-reduce.6.cloned.1.call-done = f32[128,128]{1,0:T(8,128)} async-done(((f32[128,128]{1,0:T(8,128)}), f32[128,128]{1,0:T(8,128)}) %all-reduce.6.cloned.1.call-update) | async-done | bytes 65552 | tf_op jit(solution)/shard_map/psum | solution.py:38
  285.5 2.0 gather_fusion
  287.5 0.0 copy-done
  287.5 0.2 abs_reduce_fusion.1
  287.7 0.0 copy-start.4
  287.8 0.0 copy-start.2
  287.8 58.8 %psum.45 = f32[8,128]{1,0:T(8,128)S(1)} all-reduce(f32[8,128]{1,0:T(8,128)S(1)} %bitcast.61), channel_id=1, replica_groups=mesh['vox'=32,'smp'=16] {'vox'}, use_global_device_ids=true, to_apply=%region_7.8 | all-reduce | flops 1024 | bytes 8192 | tf_op jit(solution)/shard_map/psum | solution.py:41
  346.6 0.6 reduce_max.28
  347.9 0.2 fusion.8
  348.0 0.9 fusion.21
  349.0 0.0 all-reduce.8.cloned.1.call-update
  349.0 0.0 all-reduce.10.cloned.1.call-start
  349.0 0.0 copy-done.4
  349.1 0.1 copy.22
  349.1 118.5 %all-reduce.8.cloned.1.call-done = f32[128,128]{1,0:T(8,128)} async-done(((f32[128,128]{1,0:T(8,128)}), f32[128,128]{1,0:T(8,128)}) %all-reduce.8.cloned.1.call-update) | async-done | bytes 65552 | tf_op jit(solution)/shard_map/psum | solution.py:44
  467.6 1.9 gather_fusion.1
  469.6 0.0 copy-start.9
  469.6 1.8 convolution_bitcast_fusion
  471.4 0.0 copy-done.9
  471.4 0.0 all-reduce.10.cloned.1.call-update
  471.4 0.8 copy-done.1
  472.2 0.2 abs_reduce_fusion
  472.4 0.6 reduce_max.29
  473.7 261.4 %all-reduce.10.cloned.1.call-done = f32[128,128]{1,0:T(8,128)} async-done(((f32[128,128]{1,0:T(8,128)}), f32[128,128]{1,0:T(8,128)}) %all-reduce.10.cloned.1.call-update) | async-done | bytes 65552 | tf_op jit(solution)/shard_map/psum | solution.py:50
  735.2 1.0 fusion.2
  736.2 0.3 fusion.22
  736.5 1.2 gather_fusion.2
  737.8 0.5 fusion.18
  738.3 0.6 broadcast_divide_fusion
  (13 shorter events, 0.1 us)
Async XLA Ops:
  7.2 1.8 copy-start.3
  7.2 124.6 %all-reduce.12.cloned.1.call-start = ((), (), s32[]{:S(2)}) async-start(), calls=%async_computation.3 | async-start | bytes 262144 | tf_op jit(solution)/shard_map/psum | solution.py:36
  7.2 1.7 copy-start.6
  11.2 120.6 %copy-start.10 = (f32[128]{0:T(128)S(1)}, f32[128]{0:T(128)}, u32[]{:S(2)}) copy-start(f32[128]{0:T(128)} %param.9) | copy-start | bytes 1540
  11.2 274.2 %all-reduce.6.cloned.1.call-start = ((), (), s32[]{:S(2)}) async-start(), calls=%async_computation | async-start | bytes 131072 | tf_op jit(solution)/shard_map/psum | solution.py:38
  131.8 2.6 copy-start.5
  131.8 2.6 copy-start.7
  131.8 2.6 copy-start.8
  135.7 332.0 %all-reduce.8.cloned.1.call-start = ((), (), s32[]{:S(2)}) async-start(), calls=%async_computation.1 | async-start | bytes 131072 | tf_op jit(solution)/shard_map/psum | solution.py:44
  285.5 2.0 copy-start
  287.7 61.4 %copy-start.4 = (f32[128,128]{1,0:T(8,128)}, f32[128,128]{1,0:T(8,128)S(1)}, u32[]{:S(2)}) copy-start(f32[128,128]{1,0:T(8,128)S(1)} %get-tuple-element.14) | copy-start | bytes 196612
  287.8 181.8 %copy-start.2 = (f32[128,8,128]{2,1,0:T(8,128)S(1)}, f32[128,8,128]{2,1,0:T(8,128)}, u32[]{:S(2)}) copy-start(f32[128,8,128]{2,1,0:T(8,128)} %param.5) | copy-start | bytes 1572868
  349.0 386.2 %all-reduce.10.cloned.1.call-start = ((), (), s32[]{:S(2)}) async-start(), calls=%async_computation.2 | async-start | bytes 131072 | tf_op jit(solution)/shard_map/psum | solution.py:50
  469.6 1.8 copy-start.9
  471.4 0.8 copy-start.1
Sparse Core Ops, SparseCore 0:
  11.3 120.4 all-reduce.11
  135.8 149.5 all-reduce.5
  349.1 118.4 all-reduce.7
  473.0 262.0 all-reduce.9
where the time goes:
time: 746 us; the launch traced here: 745 us
  waiting for transfers between devices  650 us (87%)
  blocking collectives  58.8 us (8%)
  between operations  16 us (2%)
  matrix products  10.6 us (1%)
    psum x1, waiting for transfers between devices, per_device(): terms_c = lax.psum(partial_c, ('vox', 'smp'))  261 us
    psum x1, waiting for transfers between devices, per_device(): gram = lax.psum(local_gram(moved), 'vox')  150 us
    psum x1, waiting for transfers between devices, per_device(): terms_a = lax.psum(partial_value, 'smp')  121 us
    psum x1, waiting for transfers between devices, per_device(): gram = lax.psum(local_gram(moved), 'smp')  118 us
    psum x1, blocking collectives, per_device(): terms_b = lax.psum(partial_b, 'vox')  58.8 us
  transfers between devices with their start and end apart: 4, of which 4 were waited for; matrix products, arithmetic and copies ran while one was open for 0% of the time, Pallas kernels for 0%

commit v1 on v0

v1 whole, which is shorter than its diff:
```python
import functools

import jax
import jax.numpy as jnp
from jax import lax
from jax.experimental import pallas as pl
from jax.experimental.pallas import tpu as pltpu
from jax.sharding import PartitionSpec as P

MESH = pl.DeviceIdType.MESH
RANK = 128
X_CHIPS = 4

GATHER_B, SCATTER_A, GATHER_A, ALONG_X, ALONG_Z, GATHER_GRAM = range(6)
GATHER_MOVED_B, SCATTER_C, ALONG_X_C, ALONG_Z_C, GATHER_C = range(6, 11)
PHASES = 11


def split(value):
    high = value.astype(jnp.bfloat16)
    low = (value - high.astype(jnp.float32)).astype(jnp.bfloat16)
    return high, low


def left_operand(value):
    return jnp.concatenate(split(value), axis=1)


def right_operand(value):
    high, low = split(value)
    return jnp.concatenate(
        [jnp.concatenate([high, low], axis=1), jnp.concatenate([high, jnp.zeros_like(low)], axis=1)], axis=0
    )


def dot_split(left, right):
    both = jnp.dot(left, right, preferred_element_type=jnp.float32)
    half = both.shape[1] // 2
    return both[:, :half] + both[:, half:]


def dot3(left, right):
    return dot_split(left_operand(left), right_operand(right))


def step_of(coupled):
    sums = jnp.sum(jnp.abs(coupled), axis=0, keepdims=True)
    return 1.0 / jnp.max(sums, axis=1, keepdims=True)


def kernel(
    x_count, z_count, s_count,
    e_in, a_in, b_in, c_in, w_in,
    a_out, b_out, c_out, w_out,
    e_v, a_v, b_v, c_v, w_v,
    contracted, e_turned, turned, partial, partial_c,
    all_b, parts_a, all_a, along_x, along_z, all_gram,
    all_moved_b, parts_c, along_x_c, along_z_c, all_c,
    load_sem, send_sem, recv_sem,
):
    vox = lax.axis_index("vox")
    me = lax.axis_index("smp")
    x = vox // z_count
    z = vox % z_count
    rows_i = a_v.shape[0] * a_v.shape[1]
    rows_j = b_v.shape[0]

    loads = [
        pltpu.make_async_copy(src, dst, load_sem.at[n])
        for n, (src, dst) in enumerate(((c_in, c_v), (b_in, b_v), (e_in, e_v), (w_in, w_v), (a_in, a_v)))
    ]
    for load in loads:
        load.start()

    def smp_peer(d):
        return {"smp": lax.rem(me + d, s_count)}

    def x_peer(d):
        return {"vox": lax.rem(x + d, x_count) * z_count + z}

    def z_peer(d):
        return {"vox": x * z_count + lax.rem(z + d, z_count)}

    barrier = pltpu.get_barrier_semaphore()
    groups = ((smp_peer, s_count), (x_peer, x_count), (z_peer, z_count))
    for peer, count in groups:
        for d in range(1, count):
            pl.semaphore_signal(barrier, inc=1, device_id=peer(d), device_id_type=MESH)

    def copy(src, dst, phase, device):
        return pltpu.make_async_remote_copy(
            src_ref=src, dst_ref=dst, send_sem=send_sem.at[phase], recv_sem=recv_sem.at[phase],
            device_id=device, device_id_type=MESH,
        )

    def gather(buffer, index, peer, count, phase):
        for d in range(1, count):
            copy(buffer.at[index], buffer.at[index], phase, peer(d)).start()

    def scatter(source, buffer, phase):
        for d in range(1, s_count):
            p = lax.rem(me + d, s_count)
            copy(source.at[p], buffer.at[me], phase, {"smp": p}).start()
        buffer[me] = source[me]

    def arrived(buffer, phase, sem=recv_sem):
        others = buffer.at[pl.ds(0, buffer.shape[0] - 1)]
        pltpu.make_async_copy(others, others, sem.at[phase]).wait()

    def whole(buffer):
        return buffer[...].reshape(buffer.shape[0] * buffer.shape[1], RANK)

    loads[0].wait()
    c = c_v[...].reshape(RANK, RANK)
    c_right = right_operand(c)
    loads[1].wait()
    loads[2].wait()
    total = jnp.zeros((rows_i, RANK), jnp.float32)
    for j in range(rows_j):
        rows = e_v[pl.ds(j, rows_i, stride=rows_j), :]
        product = dot_split(left_operand(rows), c_right)
        contracted[j] = product
        total = total + product * b_v[j : j + 1, :]
    partial[...] = total.reshape(partial.shape)
    all_b[me] = b_v[...]

    pl.semaphore_wait(barrier, sum(count - 1 for _, count in groups))
    gather(all_b, me, smp_peer, s_count, GATHER_B)
    scatter(partial, parts_a, SCATTER_A)

    loads[3].wait()
    loads[4].wait()
    w = w_v[...]
    w_pairs = jnp.broadcast_to(w, (RANK, RANK)).T * w
    w_gram_c = w_pairs * dot3(c.T, c)
    for j in range(rows_j):
        e_turned[j] = left_operand(e_v[pl.ds(j, rows_i, stride=rows_j), :].T)
    arrived(all_b, GATHER_B)
    b_all = whole(all_b)
    samples = b_all.shape[0]
    gram_b = dot3(b_all.T, b_all)
    coupled = w_gram_c * gram_b
    step = step_of(coupled)
    a_own = a_v[me]
    base = a_own - step * dot3(a_own, coupled)
    gain = step * w

    arrived(parts_a, SCATTER_A)
    moved = base + gain * jnp.sum(parts_a[...], axis=0)
    all_a[me] = moved
    gather(all_a, me, smp_peer, s_count, GATHER_A)
    arrived(all_a, GATHER_A)

    moved_a = whole(all_a)
    turned[...] = moved_a.T.reshape(turned.shape)
    a_right = right_operand(moved_a)
    chunk = turned.shape[1]
    along_x[x, :chunk, :] = dot_split(left_operand(turned[me]), a_right)
    along_x[x, chunk:, :] = jnp.concatenate(
        [jnp.sum(contracted[j] * moved_a, axis=0, keepdims=True) for j in range(rows_j)], axis=0
    )
    gather(along_x, x, x_peer, x_count, ALONG_X)
    for j in range(rows_j // 2):
        contracted[j] = dot_split(e_turned[j], a_right)
    arrived(along_x, ALONG_X)
    along_z[z] = jnp.sum(along_x[...], axis=0)
    gather(along_z, z, z_peer, z_count, ALONG_Z)
    for j in range(rows_j // 2, rows_j):
        contracted[j] = dot_split(e_turned[j], a_right)
    b_own = b_v[...]
    b_left = left_operand(b_own)
    arrived(along_z, ALONG_Z)
    summed = jnp.sum(along_z[...], axis=0)
    all_gram[me] = summed[:chunk]
    gather(all_gram, me, smp_peer, s_count, GATHER_GRAM)
    terms_b = summed[chunk:] * w
    arrived(all_gram, GATHER_GRAM)

    gram_a = whole(all_gram)
    coupled = w_gram_c * gram_a
    step = step_of(coupled)
    moved_b = b_own - step * (dot_split(b_left, right_operand(coupled)) - terms_b)
    total = contracted[0] * moved_b[0:1, :]
    for j in range(1, rows_j):
        total = total + contracted[j] * moved_b[j : j + 1, :]
    partial_c[...] = total.reshape(partial_c.shape)
    scatter(partial_c, parts_c, SCATTER_C)
    all_moved_b[me] = moved_b
    gather(all_moved_b, me, smp_peer, s_count, GATHER_MOVED_B)

    diagonal = (
        lax.broadcasted_iota(jnp.int32, (RANK, RANK), 0) == lax.broadcasted_iota(jnp.int32, (RANK, RANK), 1)
    )

    def scales_of(gram, count):
        own = jnp.sum(jnp.where(diagonal, gram, 0.0), axis=0, keepdims=True)
        return jnp.sqrt(own / count + 1e-06)

    scales_a = scales_of(gram_a, rows_i * x_count * z_count)
    a_out[...] = (moved_a / scales_a).reshape(a_out.shape)

    arrived(parts_c, SCATTER_C)
    along_x_c[x] = jnp.sum(parts_c[...], axis=0)
    gather(along_x_c, x, x_peer, x_count, ALONG_X_C)
    arrived(all_moved_b, GATHER_MOVED_B)
    b_all = whole(all_moved_b)
    gram_b = dot3(b_all.T, b_all)
    arrived(along_x_c, ALONG_X_C)
    along_z_c[z] = jnp.sum(along_x_c[...], axis=0)
    gather(along_z_c, z, z_peer, z_count, ALONG_Z_C)
    scales_b = scales_of(gram_b, samples)
    b_out[...] = moved_b / scales_b
    coupled = w_pairs * gram_a * gram_b
    step = step_of(coupled)
    c_own = c_v[me]
    base = c_own - step * dot3(c_own, coupled)
    gain = step * w
    arrived(along_z_c, ALONG_Z_C)
    all_c[me] = base + gain * jnp.sum(along_z_c[...], axis=0)
    gather(all_c, me, smp_peer, s_count, GATHER_C)
    for phase, buffer in (
        (GATHER_B, all_b), (SCATTER_A, parts_a), (GATHER_A, all_a), (ALONG_X, along_x), (ALONG_Z, along_z),
        (GATHER_GRAM, all_gram), (GATHER_MOVED_B, all_moved_b), (SCATTER_C, parts_c), (ALONG_X_C, along_x_c),
        (ALONG_Z_C, along_z_c),
    ):
        arrived(buffer, phase, send_sem)
    arrived(all_c, GATHER_C)
    moved_c = whole(all_c)
    scales_c = jnp.sqrt(jnp.sum(moved_c * moved_c, axis=0, keepdims=True) / RANK + 1e-06)
    c_out[...] = (moved_c / scales_c).reshape(c_out.shape)
    w_out[...] = w * scales_a * scales_b * scales_c
    arrived(all_c, GATHER_C, send_sem)


def per_device(x_count, z_count, s_count, ensemble, voxel_factor, sample_factor, time_factor, weights):
    rows_i, rows_j, times = ensemble.shape
    f32 = jnp.float32
    chunk_i, chunk_r = rows_i // s_count, RANK // s_count
    tiles = lambda n, rows: pltpu.VMEM((n, rows, RANK), f32)
    anywhere = pl.BlockSpec(memory_space=pl.ANY)
    vmem = pl.BlockSpec(memory_space=pltpu.VMEM)
    a, b, c, w = pl.pallas_call(
        functools.partial(kernel, x_count, z_count, s_count),
        out_shape=(
            jax.ShapeDtypeStruct((rows_i, RANK), f32),
            jax.ShapeDtypeStruct((rows_j, RANK), f32),
            jax.ShapeDtypeStruct((times, RANK), f32),
            jax.ShapeDtypeStruct((1, RANK), f32),
        ),
        in_specs=[anywhere] * 5,
        out_specs=(vmem,) * 4,
        scratch_shapes=[
            pltpu.VMEM((rows_i * rows_j, times), f32),
            tiles(s_count, chunk_i), pltpu.VMEM((rows_j, RANK), f32), tiles(s_count, chunk_r), pltpu.VMEM((1, RANK), f32),
            tiles(rows_j, rows_i), pltpu.VMEM((rows_j, times, 2 * rows_i), jnp.bfloat16),
            tiles(s_count, chunk_r), tiles(s_count, chunk_i), tiles(s_count, chunk_r),
            tiles(s_count, rows_j), tiles(s_count, chunk_i), tiles(s_count, chunk_i),
            tiles(x_count, chunk_r + rows_j), tiles(z_count, chunk_r + rows_j), tiles(s_count, chunk_r),
            tiles(s_count, rows_j), tiles(s_count, chunk_r), tiles(x_count, chunk_r), tiles(z_count, chunk_r),
            tiles(s_count, chunk_r),
            pltpu.SemaphoreType.DMA((5,)), pltpu.SemaphoreType.DMA((PHASES,)), pltpu.SemaphoreType.DMA((PHASES,)),
        ],
        compiler_params=pltpu.CompilerParams(collective_id=0, has_side_effects=True),
    )(
        ensemble.reshape(rows_i * rows_j, times),
        voxel_factor.reshape(s_count, chunk_i, RANK),
        sample_factor,
        time_factor.reshape(s_count, chunk_r, RANK),
        weights.reshape(1, RANK),
    )
    return a, b, c, w.reshape(RANK)


def solution(mesh):
    vox_count, s_count = mesh.shape["vox"], mesh.shape["smp"]
    x_count = X_CHIPS
    return jax.shard_map(
        functools.partial(per_device, x_count, vox_count // x_count, s_count),
        mesh=mesh,
        in_specs=(P("vox", "smp", None), P("vox", None), P("smp", None), P(), P()),
        out_specs=(P("vox", None), P("smp", None), P(), P()),
        check_vma=False,
    )
```

time: 746 us -> 63.9 us (0.09)
  waiting for transfers between devices: 650 us -> 0 us
  Pallas kernels: 0 us -> 59.8 us
  blocking collectives: 58.8 us -> 0 us
  between operations: 16 us -> 0.66 us
  matrix products: 10.6 us -> 0 us
    psum x4 -> x0, waiting for transfers between devices: 650 us -> none  [the longest x1 261 us: per_device(): terms_c = lax.psum(partial_c, ('vox', 'smp'))]
    pallas_call x0 -> x1, Pallas kernels: none -> 59.8 us  [per_device(): pl.pallas_call(functools.partial(kernel, x_count, z_count, s_count), out_...]
    psum x1 -> x0, blocking collectives: 58.8 us -> none  [per_device(): terms_b = lax.psum(partial_b, 'vox')]
    dot_general x10 -> x0, matrix products: 10.6 us -> none  [the longest x5 5.11 us: local_gram(): jnp.dot(moved.T, moved, precision=HIGH, preferred_element_type=jnp.float32)]
  transfers between devices with their start and end apart: 4 -> 0, of which waited for: 4 -> 0; matrix products, arithmetic and copies ran while one was open for 0% -> 0% of each run, Pallas kernels for 0% -> 0%
where the time goes in v1:
time: 63.9 us; the launch traced here: 63.7 us
  Pallas kernels  59.8 us (94%)
  local copies, waits for them, and re-layouts  3.25 us (5%)
  between operations  0.66 us (1%)
    pallas_call x1, Pallas kernels, per_device(): pl.pallas_call(functools.partial(kernel, x_count, z_count, s_count), out_...  59.8 us
    unnamed x10, local copies, waits for them, and re-layouts  3.25 us

profile of v1, /device:TPU:1, one launch (start us, length us, event | category | flops | bytes accessed | tf_op | source)
XLA Modules:
  0.0 63.7 jit_solution(2054101271521184937)
XLA Ops:
  0.6 59.8 %shard_map.84 = (f32[128,128]{1,0:T(8,128)}, f32[8,128]{1,0:T(8,128)}, f32[128,128]{1,0:T(8,128)}, f32[1,128]{1,0:T(1,128)}) custom-call(f32[1024,128]{1,0:T(8,128)} %bitcast.5, f32[16,8,128]{2,1,0:T(8,128)} %bitcast.6, f32[8,128]{1,0:T(8,128)} %b_in.1, f32[16,8,128]{2,1,0:T(8,128)} %bitcast.7, f32[1,128]{1,0:T(1,128)} %bitcast.8), custom_call_target="tpu_custom_call" | custom-call | tf_op jit(solution)/shard_map/pallas_call | solution.py:242
  60.4 0.0 copy-start.1
  60.4 0.0 copy-start
  60.4 1.5 %copy.13 = f32[128,128]{1,0:T(8,128)} copy(f32[128,128]{1,0:T(8,128)} %get-tuple-element.16) | data formatting | bytes 131072
  61.9 0.0 copy-done.1
  61.9 0.6 copy.14
  62.5 0.0 copy-done
  62.5 0.0 copy-start.2
  62.5 0.6 copy.15
  63.2 0.0 copy-done.2
  63.2 0.5 copy.16
Async XLA Ops:
  60.4 1.5 %copy-start.1 = (f32[8,128]{1,0:T(8,128)S(1)}, f32[8,128]{1,0:T(8,128)}, u32[]{:S(2)}) copy-start(f32[8,128]{1,0:T(8,128)} %get-tuple-element.17) | copy-start | bytes 12292
  60.4 2.1 %copy-start = (f32[128,128]{1,0:T(8,128)S(1)}, f32[128,128]{1,0:T(8,128)}, u32[]{:S(2)}) copy-start(f32[128,128]{1,0:T(8,128)} %get-tuple-element.18) | copy-start | bytes 196612
  62.5 0.6 copy-start.2

commit v2 on v1

v2 whole, which is shorter than its diff:
```python
import functools

import jax
import jax.numpy as jnp
from jax import lax
from jax.experimental import pallas as pl
from jax.experimental.pallas import tpu as pltpu
from jax.sharding import PartitionSpec as P

MESH = pl.DeviceIdType.MESH
RANK = 128
X_CHIPS = 4

PAIR_A, LINE_A, MOVED_A, LINE_B, PAIR_B, GRAM_SCATTER, GRAM_Z, GRAM_GATHER = range(8)
TERMS_X, TERMS_Z, LINE_MOVED_B, PAIR_MOVED_B, TIME_SCATTER, TIME_Y, TIME_Z, TIME_GATHER = range(8, 16)
EXCHANGES = 16


def split(value):
    high = value.astype(jnp.bfloat16)
    low = (value - high.astype(jnp.float32)).astype(jnp.bfloat16)
    return high, low


def left_operand(value):
    return jnp.concatenate(split(value), axis=1)


def right_operand(value):
    high, low = split(value)
    return jnp.concatenate(
        [jnp.concatenate([high, low], axis=1), jnp.concatenate([high, jnp.zeros_like(low)], axis=1)], axis=0
    )


def dot_split(left, right):
    both = jnp.dot(left, right, preferred_element_type=jnp.float32)
    half = both.shape[1] // 2
    return both[:, :half] + both[:, half:]


def dot3(left, right):
    return dot_split(left_operand(left), right_operand(right))


def step_of(coupled):
    sums = jnp.sum(jnp.abs(coupled), axis=0, keepdims=True)
    return 1.0 / jnp.max(sums, axis=1, keepdims=True)


def kernel(
    x_count, y_count, z_count,
    e_in, a_in, b_in, c_in, w_in,
    a_out, b_out, c_out, w_out,
    e_v, a_v, b_v, c_v, w_v,
    contracted, e_turned,
    part_a, pair_a, line_a, moved_halves, line_b,
    gram_part, gram_got, gram_z, gram_all, terms_x, terms_z,
    line_moved_b, time_part, time_got, time_y, time_z, time_all,
    load_sem, send_sem, recv_sem,
):
    vox = lax.axis_index("vox")
    smp = lax.axis_index("smp")
    x = vox // z_count
    z = vox % z_count
    y = smp // 2
    core = smp % 2
    block_count = 2 * x_count
    block = 2 * x + core
    rows_i = a_v.shape[0] * a_v.shape[1]
    rows_j = b_v.shape[0]

    loads = [
        pltpu.make_async_copy(src, dst, load_sem.at[n])
        for n, (src, dst) in enumerate(((c_in, c_v), (b_in, b_v), (e_in, e_v), (w_in, w_v), (a_in, a_v)))
    ]
    for load in loads:
        load.start()

    partner = {"smp": 2 * y + 1 - core}

    def y_peer(d):
        return {"smp": 2 * lax.rem(y + d, y_count) + core}

    def z_peer(d):
        return {"vox": x * z_count + lax.rem(z + d, z_count)}

    def x_peer(d):
        return {"vox": lax.rem(x + d, x_count) * z_count + z}

    def block_peer(d):
        other = lax.rem(block + d, block_count)
        return {"vox": (other // 2) * z_count + z, "smp": 2 * y + other % 2}

    barrier = pltpu.get_barrier_semaphore()
    greeted = [y_peer(d) for d in range(1, y_count)] + [z_peer(d) for d in range(1, z_count)]
    greeted += [block_peer(d) for d in range(1, block_count)]
    for peer in greeted:
        pl.semaphore_signal(barrier, inc=1, device_id=peer, device_id_type=MESH)

    def copy(src, dst, exchange, device):
        pltpu.make_async_remote_copy(
            src_ref=src, dst_ref=dst, send_sem=send_sem.at[exchange], recv_sem=recv_sem.at[exchange],
            device_id=device, device_id_type=MESH,
        ).start()

    def gather(buffer, index, peer, exchange):
        for d in range(1, buffer.shape[0]):
            copy(buffer.at[index], buffer.at[index], exchange, peer(d))

    def scatter(source, buffer, exchange):
        for d in range(1, block_count):
            copy(source.at[lax.rem(block + d, block_count)], buffer.at[block], exchange, block_peer(d))
        buffer[block] = source[block]

    def take(ref, exchange, sem=recv_sem):
        pltpu.make_async_copy(ref, ref, sem.at[exchange]).wait()

    def others(buffer):
        return buffer.at[pl.ds(0, buffer.shape[0] - 1)]

    def whole(buffer):
        return buffer[...].reshape(-1, RANK)

    loads[0].wait()
    c = whole(c_v)
    c_right = right_operand(c)
    loads[1].wait()
    loads[2].wait()
    total = jnp.zeros((rows_i, RANK), jnp.float32)
    for j in range(rows_j):
        product = dot_split(left_operand(e_v[pl.ds(j, rows_i, stride=rows_j), :]), c_right)
        contracted[j] = product
        total = total + product * b_v[j : j + 1, :]
    part_a[...] = total.reshape(part_a.shape)
    line_b[core, y] = b_v[...]

    pl.semaphore_wait(barrier, len(greeted))
    copy(part_a.at[1 - core], pair_a, PAIR_A, partner)
    gather_line(copy, line_b, core, y, y_count, y_peer, LINE_B)
    take(pair_a, PAIR_A)
    line_a[y] = part_a[core] + pair_a[...]
    gather(line_a, y, y_peer, LINE_A)

    loads[3].wait()
    loads[4].wait()
    w = w_v[...]
    w_pairs = jnp.broadcast_to(w, (RANK, RANK)).T * w
    w_gram_c = w_pairs * dot3(c.T, c)
    take(line_b.at[0, pl.ds(0, y_count - 1)], LINE_B)
    copy(line_b.at[core], line_b.at[core], PAIR_B, partner)
    for j in range(rows_j):
        e_turned[j] = left_operand(e_v[pl.ds(j, rows_i, stride=rows_j), :].T)
    take(line_b.at[0], PAIR_B)
    b_all = whole(line_b)
    samples = b_all.shape[0]
    coupled = w_gram_c * dot3(b_all.T, b_all)
    step = step_of(coupled)
    a_own = a_v[core]
    base = a_own - step * dot3(a_own, coupled)
    gain = step * w
    take(others(line_a), LINE_A)
    moved = base + gain * jnp.sum(line_a[...], axis=0)

    moved_halves[core] = moved
    copy(moved_halves.at[core], moved_halves.at[core], MOVED_A, partner)
    gram_part[...] = dot3(moved.T, moved).reshape(gram_part.shape)
    scatter(gram_part, gram_got, GRAM_SCATTER)
    take(moved_halves.at[0], MOVED_A)
    moved_a = whole(moved_halves)
    terms_x[x] = jnp.concatenate(
        [jnp.sum(contracted[j] * moved_a, axis=0, keepdims=True) for j in range(rows_j)], axis=0
    )
    gather(terms_x, x, x_peer, TERMS_X)
    a_right = right_operand(moved_a)
    take(others(gram_got), GRAM_SCATTER)
    gram_z[z] = jnp.sum(gram_got[...], axis=0)
    gather(gram_z, z, z_peer, GRAM_Z)
    take(others(terms_x), TERMS_X)
    terms_z[z] = jnp.sum(terms_x[...], axis=0)
    gather(terms_z, z, z_peer, TERMS_Z)
    for j in range(rows_j):
        contracted[j] = dot_split(e_turned[j], a_right)
    b_own = b_v[...]
    b_left = left_operand(b_own)
    take(others(gram_z), GRAM_Z)
    gram_all[block] = jnp.sum(gram_z[...], axis=0)
    gather(gram_all, block, block_peer, GRAM_GATHER)
    take(others(terms_z), TERMS_Z)
    terms_b = jnp.sum(terms_z[...], axis=0) * w
    take(others(gram_all), GRAM_GATHER)

    gram_a = whole(gram_all)
    coupled = w_gram_c * gram_a
    step = step_of(coupled)
    moved_b = b_own - step * (dot_split(b_left, right_operand(coupled)) - terms_b)
    total = contracted[0] * moved_b[0:1, :]
    for j in range(1, rows_j):
        total = total + contracted[j] * moved_b[j : j + 1, :]
    time_part[...] = total.reshape(time_part.shape)
    scatter(time_part, time_got, TIME_SCATTER)
    line_moved_b[core, y] = moved_b
    gather_line(copy, line_moved_b, core, y, y_count, y_peer, LINE_MOVED_B)

    diagonal = (
        lax.broadcasted_iota(jnp.int32, (RANK, RANK), 0) == lax.broadcasted_iota(jnp.int32, (RANK, RANK), 1)
    )

    def scales_of(gram, count):
        own = jnp.sum(jnp.where(diagonal, gram, 0.0), axis=0, keepdims=True)
        return jnp.sqrt(own / count + 1e-06)

    scales_a = scales_of(gram_a, rows_i * x_count * z_count)
    a_out[...] = moved_a / scales_a
    take(others(time_got), TIME_SCATTER)
    time_y[y] = jnp.sum(time_got[...], axis=0)
    gather(time_y, y, y_peer, TIME_Y)
    take(line_moved_b.at[0, pl.ds(0, y_count - 1)], LINE_MOVED_B)
    copy(line_moved_b.at[core], line_moved_b.at[core], PAIR_MOVED_B, partner)
    take(others(time_y), TIME_Y)
    time_z[z] = jnp.sum(time_y[...], axis=0)
    gather(time_z, z, z_peer, TIME_Z)
    take(line_moved_b.at[0], PAIR_MOVED_B)
    b_all = whole(line_moved_b)
    gram_b = dot3(b_all.T, b_all)
    scales_b = scales_of(gram_b, samples)
    b_out[...] = moved_b / scales_b
    coupled = w_pairs * gram_a * gram_b
    step = step_of(coupled)
    c_own = c_v[block]
    base = c_own - step * dot3(c_own, coupled)
    gain = step * w
    scales_ab = w * scales_a * scales_b
    take(others(time_z), TIME_Z)
    time_all[block] = base + gain * jnp.sum(time_z[...], axis=0)
    gather(time_all, block, block_peer, TIME_GATHER)
    for exchange, ref in (
        (PAIR_A, pair_a), (LINE_A, others(line_a)), (MOVED_A, moved_halves.at[0]),
        (LINE_B, line_b.at[0, pl.ds(0, y_count - 1)]), (PAIR_B, line_b.at[0]),
        (GRAM_SCATTER, others(gram_got)), (GRAM_Z, others(gram_z)), (GRAM_GATHER, others(gram_all)),
        (TERMS_X, others(terms_x)), (TERMS_Z, others(terms_z)),
        (LINE_MOVED_B, line_moved_b.at[0, pl.ds(0, y_count - 1)]), (PAIR_MOVED_B, line_moved_b.at[0]),
        (TIME_SCATTER, others(time_got)), (TIME_Y, others(time_y)), (TIME_Z, others(time_z)),
    ):
        take(ref, exchange, send_sem)
    take(others(time_all), TIME_GATHER)
    moved_c = whole(time_all)
    scales_c = jnp.sqrt(jnp.sum(moved_c * moved_c, axis=0, keepdims=True) / RANK + 1e-06)
    c_out[...] = moved_c / scales_c
    w_out[...] = scales_ab * scales_c
    take(others(time_all), TIME_GATHER, send_sem)


def gather_line(copy, buffer, core, y, y_count, y_peer, exchange):
    for d in range(1, y_count):
        copy(buffer.at[core, y], buffer.at[core, y], exchange, y_peer(d))


def store(*refs):
    count = (len(refs) - 1) // 2
    copies = [pltpu.make_async_copy(refs[n], refs[count + n], refs[-1].at[n]) for n in range(count)]
    for one in copies:
        one.start()
    for one in copies:
        one.wait()


def per_device(x_count, y_count, z_count, ensemble, voxel_factor, sample_factor, time_factor, weights):
    rows_i, rows_j, times = ensemble.shape
    f32 = jnp.float32
    half, blocks = rows_i // 2, 2 * x_count
    rows = RANK // blocks
    tiles = lambda *shape: pltpu.VMEM((*shape, RANK), f32)
    hbm = pl.BlockSpec(memory_space=pltpu.HBM)
    vmem = pl.BlockSpec(memory_space=pltpu.VMEM)
    shapes = tuple(jax.ShapeDtypeStruct((n, RANK), f32) for n in (rows_i, rows_j, times, 1))
    results = pl.pallas_call(
        functools.partial(kernel, x_count, y_count, z_count),
        out_shape=shapes,
        in_specs=[hbm] * 5,
        out_specs=(vmem,) * 4,
        scratch_shapes=[
            tiles(rows_i * rows_j), tiles(2, half), tiles(rows_j), tiles(blocks, rows), tiles(1),
            tiles(rows_j, rows_i), pltpu.VMEM((rows_j, times, 2 * rows_i), jnp.bfloat16),
            tiles(2, half), tiles(half), tiles(y_count, half), tiles(2, half), tiles(2, y_count, rows_j),
            tiles(blocks, rows), tiles(blocks, rows), tiles(z_count, rows), tiles(blocks, rows),
            tiles(x_count, rows_j), tiles(z_count, rows_j),
            tiles(2, y_count, rows_j), tiles(blocks, rows), tiles(blocks, rows), tiles(y_count, rows),
            tiles(z_count, rows), tiles(blocks, rows),
            pltpu.SemaphoreType.DMA((5,)), pltpu.SemaphoreType.DMA((EXCHANGES,)), pltpu.SemaphoreType.DMA((EXCHANGES,)),
        ],
        compiler_params=pltpu.CompilerParams(collective_id=0, has_side_effects=True, vmem_limit_bytes=16 << 20),
    )(*(pltpu.with_memory_space_constraint(value, pltpu.HBM) for value in (
        ensemble.reshape(rows_i * rows_j, times),
        voxel_factor.reshape(2, half, RANK),
        sample_factor,
        time_factor.reshape(blocks, rows, RANK),
        weights.reshape(1, RANK),
    )))
    a, b, c, w = pl.pallas_call(
        store,
        out_shape=shapes,
        in_specs=[vmem] * 4,
        out_specs=(hbm,) * 4,
        scratch_shapes=[pltpu.SemaphoreType.DMA((4,))],
        compiler_params=pltpu.CompilerParams(vmem_limit_bytes=1 << 20),
    )(*results)
    return a, b, c, w.reshape(RANK)


def solution(mesh):
    vox_count, y_count = mesh.shape["vox"], mesh.shape["smp"] // 2
    x_count = X_CHIPS
    return jax.shard_map(
        functools.partial(per_device, x_count, y_count, vox_count // x_count),
        mesh=mesh,
        in_specs=(P("vox", "smp", None), P("vox", None), P("smp", None), P(), P()),
        out_specs=(P("vox", None), P("smp", None), P(), P()),
        check_vma=False,
    )
```

time: 63.9 us -> 56.5 us (0.88)
  Pallas kernels: 59.8 us -> 55.7 us
  local copies, waits for them, and re-layouts: 3.25 us -> 0 us
    pallas_call x1 -> x2, Pallas kernels: 59.8 us -> 55.7 us  [the longest x1 55 us: per_device(): pl.pallas_call(functools.partial(kernel, x_count, y_count, z_count), out_...]
    unnamed x10 -> x0, local copies, waits for them, and re-layouts: 3.25 us -> none
where the time goes in v2:
time: 56.5 us; the launch traced here: 56.4 us
  Pallas kernels  55.7 us (99%)
  between operations  0.64 us (1%)
    pallas_call x1, Pallas kernels, per_device(): pl.pallas_call(functools.partial(kernel, x_count, y_count, z_count), out_...  55 us

profile of v2, /device:TPU:1, one launch (start us, length us, event | category | flops | bytes accessed | tf_op | source)
XLA Modules:
  0.0 56.4 jit_solution(18307020698039132136)
XLA Ops:
  0.6 55.0 %shard_map.84 = (f32[128,128]{1,0:T(8,128)S(1)}, f32[8,128]{1,0:T(8,128)S(1)}, f32[128,128]{1,0:T(8,128)S(1)}, f32[1,128]{1,0:T(1,128)S(1)}) custom-call(f32[1024,128]{1,0:T(8,128)} %bitcast.5, f32[2,64,128]{2,1,0:T(8,128)} %bitcast.6, f32[8,128]{1,0:T(8,128)} %b_in.1, f32[8,16,128]{2,1,0:T(8,128)} %bitcast.7, f32[1,128]{1,0:T(1,128)} %bitcast.8), custom_call_target="tpu_custom_call" | custom-call | tf_op jit(solution)/shard_map/pallas_call | solution.py:277
  55.7 0.7 %shard_map.85 = (f32[128,128]{1,0:T(8,128)}, f32[8,128]{1,0:T(8,128)}, f32[128,128]{1,0:T(8,128)}, f32[1,128]{1,0:T(1,128)}) custom-call(f32[128,128]{1,0:T(8,128)S(1)} %get-tuple-element.12.refs_0_, f32[8,128]{1,0:T(8,128)S(1)} %get-tuple-element.13.refs_1_, f32[128,128]{1,0:T(8,128)S(1)} %get-tuple-element.14.refs_2_, f32[1,128]{1,0:T(1,128)S(1)} %get-tuple-element.15.refs_3_), custom_call_target="tpu_custom_call" | custom-call | tf_op jit(solution)/shard_map/pallas_call | solution.py:300

commit v3 on v2

--- a/solution.py
+++ b/solution.py
@@ -12,8 +12,9 @@
 X_CHIPS = 4
 
 PAIR_A, LINE_A, MOVED_A, LINE_B, PAIR_B, GRAM_SCATTER, GRAM_Z, GRAM_GATHER = range(8)
-TERMS_X, TERMS_Z, LINE_MOVED_B, PAIR_MOVED_B, TIME_SCATTER, TIME_Y, TIME_Z, TIME_GATHER = range(8, 16)
-EXCHANGES = 16
+TERMS_X, TERMS_Z, TERMS_PAIR, STRIPS, LINE_FIXED, LINE_STEP = range(8, 14)
+LINE_MOVED_B, PAIR_MOVED_B, TIME_Z, TIME_GATHER = range(14, 18)
+EXCHANGES = 18
 
 
 def split(value):
@@ -53,10 +54,12 @@
     e_in, a_in, b_in, c_in, w_in,
     a_out, b_out, c_out, w_out,
     e_v, a_v, b_v, c_v, w_v,
-    contracted, e_turned,
+    contracted, e_right,
     part_a, pair_a, line_a, moved_halves, line_b,
-    gram_part, gram_got, gram_z, gram_all, terms_x, terms_z,
-    line_moved_b, time_part, time_got, time_y, time_z, time_all,
+    gram_part, gram_got, gram_z, gram_all, terms_x, terms_z, terms_pair,
+    strips, strips_got, strip_terms, by_rank, w_gram_c_v, w_turned, base_v,
+    fixed_line, step_line,
+    line_moved_b, time_z, time_all,
     load_sem, send_sem, recv_sem,
 ):
     vox = lax.axis_index("vox")
@@ -67,6 +70,7 @@
     core = smp % 2
     block_count = 2 * x_count
     block = 2 * x + core
+    strip = RANK // block_count
     rows_i = a_v.shape[0] * a_v.shape[1]
     rows_j = b_v.shape[0]
 
@@ -145,13 +149,26 @@
     loads[3].wait()
     loads[4].wait()
     w = w_v[...]
-    w_pairs = jnp.broadcast_to(w, (RANK, RANK)).T * w
+    w_columns = jnp.broadcast_to(w, (RANK, RANK)).T
+    w_turned[...] = w_columns.reshape(w_turned.shape)
+    w_pairs = w_columns * w
     w_gram_c = w_pairs * dot3(c.T, c)
+    w_gram_c_v[...] = w_gram_c.reshape(w_gram_c_v.shape)
+    b_own = b_v[...]
+    b_left = left_operand(b_own)
+
+    def turn(own, partners):
+        filler = jnp.zeros((RANK - 2 * rows_j, RANK), jnp.float32)
+        return jnp.concatenate([own, partners, filler], axis=0).T
+
     take(line_b.at[0, pl.ds(0, y_count - 1)], LINE_B)
     copy(line_b.at[core], line_b.at[core], PAIR_B, partner)
     for j in range(rows_j):
-        e_turned[j] = left_operand(e_v[pl.ds(j, rows_i, stride=rows_j), :].T)
+        e_right[j] = right_operand(e_v[pl.ds(j, rows_i, stride=rows_j), :])
     take(line_b.at[0], PAIR_B)
+    b_turned = turn(b_own, line_b[1 - core, y])
+    b_turned_right = right_operand(b_turned)
+    by_rank[0] = b_turned.reshape(by_rank.shape[1:])
     b_all = whole(line_b)
     samples = b_all.shape[0]
     coupled = w_gram_c * dot3(b_all.T, b_all)
@@ -172,35 +189,64 @@
         [jnp.sum(contracted[j] * moved_a, axis=0, keepdims=True) for j in range(rows_j)], axis=0
     )
     gather(terms_x, x, x_peer, TERMS_X)
-    a_right = right_operand(moved_a)
+
+    a_left = left_operand(moved_a.T)
+    for j in range(rows_j):
+        strips[:, j] = dot_split(a_left, e_right[j]).reshape(block_count, strip, RANK)
+    for d in range(1, block_count):
+        copy(strips.at[lax.rem(block + d, block_count)], strips_got.at[d - 1], STRIPS, block_peer(d))
     take(others(gram_got), GRAM_SCATTER)
     gram_z[z] = jnp.sum(gram_got[...], axis=0)
     gather(gram_z, z, z_peer, GRAM_Z)
     take(others(terms_x), TERMS_X)
     terms_z[z] = jnp.sum(terms_x[...], axis=0)
     gather(terms_z, z, z_peer, TERMS_Z)
-    for j in range(rows_j):
-        contracted[j] = dot_split(e_turned[j], a_right)
-    b_own = b_v[...]
-    b_left = left_operand(b_own)
-    take(others(gram_z), GRAM_Z)
-    gram_all[block] = jnp.sum(gram_z[...], axis=0)
-    gather(gram_all, block, block_peer, GRAM_GATHER)
     take(others(terms_z), TERMS_Z)
     terms_b = jnp.sum(terms_z[...], axis=0) * w
+    terms_pair[core] = terms_b
+    copy(terms_pair.at[core], terms_pair.at[core], TERMS_PAIR, partner)
+    take(others(gram_z), GRAM_Z)
+    gram_strip = jnp.sum(gram_z[...], axis=0)
+    gram_all[block] = gram_strip
+    gather(gram_all, block, block_peer, GRAM_GATHER)
+    take(strips_got, STRIPS)
+
+    for j in range(rows_j):
+        own, partners = strips[block, j], strips_got[0, j]
+        for d in range(2, block_count):
+            if d % 2:
+                partners = partners + strips_got[d - 1, j]
+            else:
+                own = own + strips_got[d - 1, j]
+        strip_terms[j] = own
+        strip_terms[rows_j + j] = partners
+
+    def mix(samples_in_lanes):
+        total = strip_terms[0] * samples_in_lanes[:, 0:1]
+        for j in range(1, 2 * rows_j):
+            total = total + strip_terms[j] * samples_in_lanes[:, j : j + 1]
+        return total
+
+    fixed_line[y] = mix(by_rank[0, block])
+    gather(fixed_line, y, y_peer, LINE_FIXED)
+    take(terms_pair.at[0], TERMS_PAIR)
+    by_rank[1] = turn(terms_b, terms_pair[1 - core]).reshape(by_rank.shape[1:])
+    pull = dot_split(left_operand(w_gram_c_v[block] * gram_strip), b_turned_right) - by_rank[1, block]
+    step_line[y] = mix(pull)
+    gather(step_line, y, y_peer, LINE_STEP)
+
     take(others(gram_all), GRAM_GATHER)
-
     gram_a = whole(gram_all)
     coupled = w_gram_c * gram_a
-    step = step_of(coupled)
-    moved_b = b_own - step * (dot_split(b_left, right_operand(coupled)) - terms_b)
-    total = contracted[0] * moved_b[0:1, :]
-    for j in range(1, rows_j):
-        total = total + contracted[j] * moved_b[j : j + 1, :]
-    time_part[...] = total.reshape(time_part.shape)
-    scatter(time_part, time_got, TIME_SCATTER)
+    step_b = step_of(coupled)
+    moved_b = b_own - step_b * (dot_split(b_left, right_operand(coupled)) - terms_b)
     line_moved_b[core, y] = moved_b
     gather_line(copy, line_moved_b, core, y, y_count, y_peer, LINE_MOVED_B)
+    take(others(fixed_line), LINE_FIXED)
+    fixed = jnp.sum(fixed_line[...], axis=0)
+    take(others(step_line), LINE_STEP)
+    time_z[z] = fixed - step_b * jnp.sum(step_line[...], axis=0)
+    gather(time_z, z, z_peer, TIME_Z)
 
     diagonal = (
         lax.broadcasted_iota(jnp.int32, (RANK, RANK), 0) == lax.broadcasted_iota(jnp.int32, (RANK, RANK), 1)
@@ -210,41 +256,36 @@
         own = jnp.sum(jnp.where(diagonal, gram, 0.0), axis=0, keepdims=True)
         return jnp.sqrt(own / count + 1e-06)
 
+    take(line_moved_b.at[0, pl.ds(0, y_count - 1)], LINE_MOVED_B)
+    copy(line_moved_b.at[core], line_moved_b.at[core], PAIR_MOVED_B, partner)
     scales_a = scales_of(gram_a, rows_i * x_count * z_count)
     a_out[...] = moved_a / scales_a
-    take(others(time_got), TIME_SCATTER)
-    time_y[y] = jnp.sum(time_got[...], axis=0)
-    gather(time_y, y, y_peer, TIME_Y)
-    take(line_moved_b.at[0, pl.ds(0, y_count - 1)], LINE_MOVED_B)
-    copy(line_moved_b.at[core], line_moved_b.at[core], PAIR_MOVED_B, partner)
-    take(others(time_y), TIME_Y)
-    time_z[z] = jnp.sum(time_y[...], axis=0)
-    gather(time_z, z, z_peer, TIME_Z)
     take(line_moved_b.at[0], PAIR_MOVED_B)
     b_all = whole(line_moved_b)
     gram_b = dot3(b_all.T, b_all)
+    coupled = w_pairs * gram_a * gram_b
+    step = step_of(coupled)
+    base = c - step * dot3(c, coupled)
+    base_v[...] = base.T.reshape(base_v.shape)
+    gain = step * w_turned[block]
     scales_b = scales_of(gram_b, samples)
     b_out[...] = moved_b / scales_b
-    coupled = w_pairs * gram_a * gram_b
-    step = step_of(coupled)
-    c_own = c_v[block]
-    base = c_own - step * dot3(c_own, coupled)
-    gain = step * w
     scales_ab = w * scales_a * scales_b
     take(others(time_z), TIME_Z)
-    time_all[block] = base + gain * jnp.sum(time_z[...], axis=0)
+    time_all[block] = base_v[block] + gain * jnp.sum(time_z[...], axis=0)
     gather(time_all, block, block_peer, TIME_GATHER)
     for exchange, ref in (
         (PAIR_A, pair_a), (LINE_A, others(line_a)), (MOVED_A, moved_halves.at[0]),
         (LINE_B, line_b.at[0, pl.ds(0, y_count - 1)]), (PAIR_B, line_b.at[0]),
         (GRAM_SCATTER, others(gram_got)), (GRAM_Z, others(gram_z)), (GRAM_GATHER, others(gram_all)),
-        (TERMS_X, others(terms_x)), (TERMS_Z, others(terms_z)),
+        (TERMS_X, others(terms_x)), (TERMS_Z, others(terms_z)), (TERMS_PAIR, terms_pair.at[0]),
+        (STRIPS, strips_got), (LINE_FIXED, others(fixed_line)), (LINE_STEP, others(step_line)),
         (LINE_MOVED_B, line_moved_b.at[0, pl.ds(0, y_count - 1)]), (PAIR_MOVED_B, line_moved_b.at[0]),
-        (TIME_SCATTER, others(time_got)), (TIME_Y, others(time_y)), (TIME_Z, others(time_z)),
+        (TIME_Z, others(time_z)),
     ):
         take(ref, exchange, send_sem)
     take(others(time_all), TIME_GATHER)
-    moved_c = whole(time_all)
+    moved_c = whole(time_all).T
     scales_c = jnp.sqrt(jnp.sum(moved_c * moved_c, axis=0, keepdims=True) / RANK + 1e-06)
     c_out[...] = moved_c / scales_c
     w_out[...] = scales_ab * scales_c
@@ -281,12 +322,14 @@
         out_specs=(vmem,) * 4,
         scratch_shapes=[
             tiles(rows_i * rows_j), tiles(2, half), tiles(rows_j), tiles(blocks, rows), tiles(1),
-            tiles(rows_j, rows_i), pltpu.VMEM((rows_j, times, 2 * rows_i), jnp.bfloat16),
+            tiles(rows_j, rows_i), pltpu.VMEM((rows_j, 2 * rows_i, 2 * times), jnp.bfloat16),
             tiles(2, half), tiles(half), tiles(y_count, half), tiles(2, half), tiles(2, y_count, rows_j),
             tiles(blocks, rows), tiles(blocks, rows), tiles(z_count, rows), tiles(blocks, rows),
-            tiles(x_count, rows_j), tiles(z_count, rows_j),
-            tiles(2, y_count, rows_j), tiles(blocks, rows), tiles(blocks, rows), tiles(y_count, rows),
-            tiles(z_count, rows), tiles(blocks, rows),
+            tiles(x_count, rows_j), tiles(z_count, rows_j), tiles(2, rows_j),
+            tiles(blocks, rows_j, rows), tiles(blocks - 1, rows_j, rows), tiles(2 * rows_j, rows),
+            tiles(2, blocks, rows), tiles(blocks, rows), tiles(blocks, rows), tiles(blocks, rows),
+            tiles(y_count, rows), tiles(y_count, rows),
+            tiles(2, y_count, rows_j), tiles(z_count, rows), tiles(blocks, rows),
             pltpu.SemaphoreType.DMA((5,)), pltpu.SemaphoreType.DMA((EXCHANGES,)), pltpu.SemaphoreType.DMA((EXCHANGES,)),
         ],
         compiler_params=pltpu.CompilerParams(collective_id=0, has_side_effects=True, vmem_limit_bytes=16 << 20),

time: 56.5 us -> 51.3 us (0.908)
  Pallas kernels: 55.7 us -> 50.6 us
    pallas_call x1, Pallas kernels: 55 us -> 49.9 us  [per_device(): pl.pallas_call(functools.partial(kernel, x_count, y_count, z_count), out_...]
where the time goes in v3:
time: 51.3 us; the launch traced here: 51.2 us
  Pallas kernels  50.6 us (99%)
  between operations  0.64 us (1%)
    pallas_call x1, Pallas kernels, per_device(): pl.pallas_call(functools.partial(kernel, x_count, y_count, z_count), out_...  49.9 us

profile of v3, /device:TPU:1, one launch (start us, length us, event | category | flops | bytes accessed | tf_op | source)
XLA Modules:
  0.0 51.2 jit_solution(1287016157061935152)
XLA Ops:
  0.6 49.9 %shard_map.84 = (f32[128,128]{1,0:T(8,128)S(1)}, f32[8,128]{1,0:T(8,128)S(1)}, f32[128,128]{1,0:T(8,128)S(1)}, f32[1,128]{1,0:T(1,128)S(1)}) custom-call(f32[1024,128]{1,0:T(8,128)} %bitcast.5, f32[2,64,128]{2,1,0:T(8,128)} %bitcast.6, f32[8,128]{1,0:T(8,128)} %b_in.1, f32[8,16,128]{2,1,0:T(8,128)} %bitcast.7, f32[1,128]{1,0:T(1,128)} %bitcast.8), custom_call_target="tpu_custom_call" | custom-call | tf_op jit(solution)/shard_map/pallas_call | solution.py:318
  50.5 0.7 %shard_map.85 = (f32[128,128]{1,0:T(8,128)}, f32[8,128]{1,0:T(8,128)}, f32[128,128]{1,0:T(8,128)}, f32[1,128]{1,0:T(1,128)}) custom-call(f32[128,128]{1,0:T(8,128)S(1)} %get-tuple-element.12.refs_0_, f32[8,128]{1,0:T(8,128)S(1)} %get-tuple-element.13.refs_1_, f32[128,128]{1,0:T(8,128)S(1)} %get-tuple-element.14.refs_2_, f32[1,128]{1,0:T(1,128)S(1)} %get-tuple-element.15.refs_3_), custom_call_target="tpu_custom_call" | custom-call | tf_op jit(solution)/shard_map/pallas_call | solution.py:343

commit v4 on v3

--- a/solution.py
+++ b/solution.py
@@ -12,9 +12,9 @@
 X_CHIPS = 4
 
 PAIR_A, LINE_A, MOVED_A, LINE_B, PAIR_B, GRAM_SCATTER, GRAM_Z, GRAM_GATHER = range(8)
-TERMS_X, TERMS_Z, TERMS_PAIR, STRIPS, LINE_FIXED, LINE_STEP = range(8, 14)
-LINE_MOVED_B, PAIR_MOVED_B, TIME_Z, TIME_GATHER = range(14, 18)
-EXCHANGES = 18
+TERMS_SCATTER, TERMS_Z, TERMS_GATHER, FIXED_SCATTER, STRIPS, LINE_FIXED, LINE_STEP = range(8, 15)
+LINE_MOVED_B, PAIR_MOVED_B, TIME_Z, TIME_GATHER = range(15, 19)
+EXCHANGES = 19
 
 
 def split(value):
@@ -42,6 +42,10 @@
 
 def dot3(left, right):
     return dot_split(left_operand(left), right_operand(right))
+
+
+def far_first(count):
+    return sorted(range(1, count), key=lambda d: -min(d, count - d))
 
 
 def step_of(coupled):
@@ -56,8 +60,8 @@
     e_v, a_v, b_v, c_v, w_v,
     contracted, e_right,
     part_a, pair_a, line_a, moved_halves, line_b,
-    gram_part, gram_got, gram_z, gram_all, terms_x, terms_z, terms_pair,
-    strips, strips_got, strip_terms, by_rank, w_gram_c_v, w_turned, base_v,
+    gram_part, gram_got, gram_z, gram_all, terms_part, terms_got, terms_z, terms_all, fixed_part, fixed_got,
+    strips, strips_got, w_gram_c_v, w_turned, c_turned_v, coupled_v,
     fixed_line, step_line,
     line_moved_b, time_z, time_all,
     load_sem, send_sem, recv_sem,
@@ -76,7 +80,7 @@
 
     loads = [
         pltpu.make_async_copy(src, dst, load_sem.at[n])
-        for n, (src, dst) in enumerate(((c_in, c_v), (b_in, b_v), (e_in, e_v), (w_in, w_v), (a_in, a_v)))
+        for n, (src, dst) in enumerate(((e_in, e_v), (c_in, c_v), (b_in, b_v), (w_in, w_v), (a_in, a_v)))
     ]
     for load in loads:
         load.start()
@@ -92,13 +96,17 @@
     def x_peer(d):
         return {"vox": lax.rem(x + d, x_count) * z_count + z}
 
-    def block_peer(d):
-        other = lax.rem(block + d, block_count)
-        return {"vox": (other // 2) * z_count + z, "smp": 2 * y + other % 2}
+    def block_at(dx, flip):
+        return 2 * lax.rem(x + dx, x_count) + (1 - core if flip else core)
+
+    def block_peer(dx, flip):
+        return {"vox": lax.rem(x + dx, x_count) * z_count + z, "smp": 2 * y + (1 - core if flip else core)}
+
+    block_peers = [(dx, flip) for dx in far_first(x_count) for flip in (0, 1)] + [(0, 1)]
 
     barrier = pltpu.get_barrier_semaphore()
-    greeted = [y_peer(d) for d in range(1, y_count)] + [z_peer(d) for d in range(1, z_count)]
-    greeted += [block_peer(d) for d in range(1, block_count)]
+    greeted = [y_peer(d) for d in far_first(y_count)] + [z_peer(d) for d in far_first(z_count)]
+    greeted += [block_peer(*at) for at in block_peers]
     for peer in greeted:
         pl.semaphore_signal(barrier, inc=1, device_id=peer, device_id_type=MESH)
 
@@ -109,12 +117,16 @@
         ).start()
 
     def gather(buffer, index, peer, exchange):
-        for d in range(1, buffer.shape[0]):
+        for d in far_first(buffer.shape[0]):
             copy(buffer.at[index], buffer.at[index], exchange, peer(d))
 
+    def gather_blocks(buffer, exchange):
+        for at in block_peers:
+            copy(buffer.at[block], buffer.at[block], exchange, block_peer(*at))
+
     def scatter(source, buffer, exchange):
-        for d in range(1, block_count):
-            copy(source.at[lax.rem(block + d, block_count)], buffer.at[block], exchange, block_peer(d))
+        for at in block_peers:
+            copy(source.at[block_at(*at)], buffer.at[block], exchange, block_peer(*at))
         buffer[block] = source[block]
 
     def take(ref, exchange, sem=recv_sem):
@@ -126,11 +138,11 @@
     def whole(buffer):
         return buffer[...].reshape(-1, RANK)
 
-    loads[0].wait()
+    loads[1].wait()
     c = whole(c_v)
     c_right = right_operand(c)
-    loads[1].wait()
     loads[2].wait()
+    loads[0].wait()
     total = jnp.zeros((rows_i, RANK), jnp.float32)
     for j in range(rows_j):
         product = dot_split(left_operand(e_v[pl.ds(j, rows_i, stride=rows_j), :]), c_right)
@@ -154,6 +166,9 @@
     w_pairs = w_columns * w
     w_gram_c = w_pairs * dot3(c.T, c)
     w_gram_c_v[...] = w_gram_c.reshape(w_gram_c_v.shape)
+    c_turned = c.T
+    c_turned_right = right_operand(c_turned)
+    c_turned_v[...] = c_turned.reshape(c_turned_v.shape)
     b_own = b_v[...]
     b_left = left_operand(b_own)
 
@@ -168,7 +183,6 @@
     take(line_b.at[0], PAIR_B)
     b_turned = turn(b_own, line_b[1 - core, y])
     b_turned_right = right_operand(b_turned)
-    by_rank[0] = b_turned.reshape(by_rank.shape[1:])
     b_all = whole(line_b)
     samples = b_all.shape[0]
     coupled = w_gram_c * dot3(b_all.T, b_all)
@@ -185,56 +199,71 @@
     scatter(gram_part, gram_got, GRAM_SCATTER)
     take(moved_halves.at[0], MOVED_A)
     moved_a = whole(moved_halves)
-    terms_x[x] = jnp.concatenate(
+    raw_terms = jnp.concatenate(
         [jnp.sum(contracted[j] * moved_a, axis=0, keepdims=True) for j in range(rows_j)], axis=0
     )
-    gather(terms_x, x, x_peer, TERMS_X)
+    filler = jnp.zeros((RANK - rows_j, RANK), jnp.float32)
+    packed = pack(jnp.concatenate([raw_terms, filler], axis=0).T, strip, rows_j)
+    for n in range(block_count):
+        terms_part[n] = packed[n]
+    for n, at in enumerate(block_peers):
+        copy(terms_part.at[block_at(*at)], terms_got.at[n], TERMS_SCATTER, block_peer(*at))
 
     a_left = left_operand(moved_a.T)
+    fixed = jnp.zeros((RANK, RANK), jnp.float32)
     for j in range(rows_j):
-        strips[:, j] = dot_split(a_left, e_right[j]).reshape(block_count, strip, RANK)
-    for d in range(1, block_count):
-        copy(strips.at[lax.rem(block + d, block_count)], strips_got.at[d - 1], STRIPS, block_peer(d))
+        product = dot_split(a_left, e_right[j])
+        strips[:, j] = product.reshape(block_count, strip, RANK)
+        fixed = fixed + product * b_turned[:, j : j + 1]
+    fixed_part[...] = fixed.reshape(fixed_part.shape)
+    scatter(fixed_part, fixed_got, FIXED_SCATTER)
+    for n, at in enumerate(block_peers):
+        copy(strips.at[block_at(*at)], strips_got.at[n], STRIPS, block_peer(*at))
     take(others(gram_got), GRAM_SCATTER)
     gram_z[z] = jnp.sum(gram_got[...], axis=0)
     gather(gram_z, z, z_peer, GRAM_Z)
-    take(others(terms_x), TERMS_X)
-    terms_z[z] = jnp.sum(terms_x[...], axis=0)
+    take(terms_got, TERMS_SCATTER)
+    by_core = [terms_part[block], jnp.zeros_like(terms_part[0])]
+    for n, (_, flip) in enumerate(block_peers):
+        by_core[flip] = by_core[flip] + terms_got[n]
+    terms_z[z] = jnp.concatenate(by_core, axis=0)
     gather(terms_z, z, z_peer, TERMS_Z)
-    take(others(terms_z), TERMS_Z)
-    terms_b = jnp.sum(terms_z[...], axis=0) * w
-    terms_pair[core] = terms_b
-    copy(terms_pair.at[core], terms_pair.at[core], TERMS_PAIR, partner)
+    take(others(fixed_got), FIXED_SCATTER)
+    fixed_line[y] = jnp.sum(fixed_got[...], axis=0)
+    gather(fixed_line, y, y_peer, LINE_FIXED)
     take(others(gram_z), GRAM_Z)
     gram_strip = jnp.sum(gram_z[...], axis=0)
     gram_all[block] = gram_strip
-    gather(gram_all, block, block_peer, GRAM_GATHER)
+    gather_blocks(gram_all, GRAM_GATHER)
+
+    pull = dot_split(left_operand(w_gram_c_v[block] * gram_strip), b_turned_right)
+    take(others(terms_z), TERMS_Z)
+    terms = jnp.sum(terms_z[...], axis=0)
+    terms_all[block, pl.ds(core, 1), :] = terms[0:1]
+    terms_all[block, pl.ds(1 - core, 1), :] = terms[1:2]
+    gather_blocks(terms_all, TERMS_GATHER)
+    lanes = lax.broadcasted_iota(jnp.int32, (strip, RANK), 1)
+    strip_terms = jnp.where(
+        lanes < rows_j, unpack(terms[0:1], strip, rows_j, 0), unpack(terms[1:2], strip, rows_j, rows_j)
+    )
+    pull = pull - strip_terms * w_turned[block]
     take(strips_got, STRIPS)
-
+    total = None
     for j in range(rows_j):
-        own, partners = strips[block, j], strips_got[0, j]
-        for d in range(2, block_count):
-            if d % 2:
-                partners = partners + strips_got[d - 1, j]
-            else:
-                own = own + strips_got[d - 1, j]
-        strip_terms[j] = own
-        strip_terms[rows_j + j] = partners
-
-    def mix(samples_in_lanes):
-        total = strip_terms[0] * samples_in_lanes[:, 0:1]
-        for j in range(1, 2 * rows_j):
-            total = total + strip_terms[j] * samples_in_lanes[:, j : j + 1]
-        return total
-
-    fixed_line[y] = mix(by_rank[0, block])
-    gather(fixed_line, y, y_peer, LINE_FIXED)
-    take(terms_pair.at[0], TERMS_PAIR)
-    by_rank[1] = turn(terms_b, terms_pair[1 - core]).reshape(by_rank.shape[1:])
-    pull = dot_split(left_operand(w_gram_c_v[block] * gram_strip), b_turned_right) - by_rank[1, block]
-    step_line[y] = mix(pull)
+        by_core = [strips[block, j], None]
+        for n, (_, flip) in enumerate(block_peers):
+            got = strips_got[n, j]
+            by_core[flip] = got if by_core[flip] is None else by_core[flip] + got
+        term = by_core[0] * pull[:, j : j + 1] + by_core[1] * pull[:, rows_j + j : rows_j + j + 1]
+        total = term if total is None else total + term
+    step_line[y] = total
     gather(step_line, y, y_peer, LINE_STEP)
 
+    take(others(terms_all), TERMS_GATHER)
+    columns = [
+        unpack(terms_all[n, pl.ds(core, 1), :], strip, rows_j, 0) for n in range(block_count)
+    ]
+    terms_b = jnp.concatenate(columns, axis=0).T[:rows_j] * w
     take(others(gram_all), GRAM_GATHER)
     gram_a = whole(gram_all)
     coupled = w_gram_c * gram_a
@@ -258,27 +287,28 @@
 
     take(line_moved_b.at[0, pl.ds(0, y_count - 1)], LINE_MOVED_B)
     copy(line_moved_b.at[core], line_moved_b.at[core], PAIR_MOVED_B, partner)
+    w_gram_a = w_pairs * gram_a
     scales_a = scales_of(gram_a, rows_i * x_count * z_count)
     a_out[...] = moved_a / scales_a
     take(line_moved_b.at[0], PAIR_MOVED_B)
     b_all = whole(line_moved_b)
     gram_b = dot3(b_all.T, b_all)
-    coupled = w_pairs * gram_a * gram_b
+    coupled = w_gram_a * gram_b
+    coupled_v[...] = coupled.reshape(coupled_v.shape)
     step = step_of(coupled)
-    base = c - step * dot3(c, coupled)
-    base_v[...] = base.T.reshape(base_v.shape)
+    base = c_turned_v[block] - step * dot_split(left_operand(coupled_v[block]), c_turned_right)
     gain = step * w_turned[block]
     scales_b = scales_of(gram_b, samples)
     b_out[...] = moved_b / scales_b
     scales_ab = w * scales_a * scales_b
     take(others(time_z), TIME_Z)
-    time_all[block] = base_v[block] + gain * jnp.sum(time_z[...], axis=0)
-    gather(time_all, block, block_peer, TIME_GATHER)
+    time_all[block] = base + gain * jnp.sum(time_z[...], axis=0)
+    gather_blocks(time_all, TIME_GATHER)
     for exchange, ref in (
         (PAIR_A, pair_a), (LINE_A, others(line_a)), (MOVED_A, moved_halves.at[0]),
         (LINE_B, line_b.at[0, pl.ds(0, y_count - 1)]), (PAIR_B, line_b.at[0]),
         (GRAM_SCATTER, others(gram_got)), (GRAM_Z, others(gram_z)), (GRAM_GATHER, others(gram_all)),
-        (TERMS_X, others(terms_x)), (TERMS_Z, others(terms_z)), (TERMS_PAIR, terms_pair.at[0]),
+        (TERMS_SCATTER, terms_got), (TERMS_Z, others(terms_z)), (TERMS_GATHER, others(terms_all)), (FIXED_SCATTER, others(fixed_got)),
         (STRIPS, strips_got), (LINE_FIXED, others(fixed_line)), (LINE_STEP, others(step_line)),
         (LINE_MOVED_B, line_moved_b.at[0, pl.ds(0, y_count - 1)]), (PAIR_MOVED_B, line_moved_b.at[0]),
         (TIME_Z, others(time_z)),
@@ -292,8 +322,33 @@
     take(others(time_all), TIME_GATHER, send_sem)
 
 
+def slide(value, first, each):
+    value = pltpu.roll(value, first % RANK, 1) if first % RANK else value
+    row = lax.broadcasted_iota(jnp.int32, value.shape, 0)
+    for bit in (1, 2, 4):
+        value = jnp.where((row & bit) != 0, pltpu.roll(value, bit * each % RANK, 1), value)
+    return value
+
+
+def pack(columns, strip, count):
+    rows = []
+    for start in range(0, RANK, strip):
+        row = None
+        for n in range(0, strip, 8):
+            tile = slide(columns[start + n : start + n + 8], n * count, count)
+            part = jnp.sum(tile, axis=0, keepdims=True)
+            row = part if row is None else row + part
+        rows.append(row)
+    return rows
+
+
+def unpack(row, strip, count, lane):
+    tile = jnp.broadcast_to(row, (8, RANK))
+    return jnp.concatenate([slide(tile, lane - n * count, -count) for n in range(0, strip, 8)], axis=0)
+
+
 def gather_line(copy, buffer, core, y, y_count, y_peer, exchange):
-    for d in range(1, y_count):
+    for d in far_first(y_count):
         copy(buffer.at[core, y], buffer.at[core, y], exchange, y_peer(d))
 
 
@@ -325,9 +380,8 @@
             tiles(rows_j, rows_i), pltpu.VMEM((rows_j, 2 * rows_i, 2 * times), jnp.bfloat16),
             tiles(2, half), tiles(half), tiles(y_count, half), tiles(2, half), tiles(2, y_count, rows_j),
             tiles(blocks, rows), tiles(blocks, rows), tiles(z_count, rows), tiles(blocks, rows),
-            tiles(x_count, rows_j), tiles(z_count, rows_j), tiles(2, rows_j),
-            tiles(blocks, rows_j, rows), tiles(blocks - 1, rows_j, rows), tiles(2 * rows_j, rows),
-            tiles(2, blocks, rows), tiles(blocks, rows), tiles(blocks, rows), tiles(blocks, rows),
+            tiles(blocks, 1), tiles(blocks - 1, 1), tiles(z_count, 2), tiles(blocks, 2), tiles(blocks, rows), tiles(blocks, rows),
+            tiles(blocks, rows_j, rows), tiles(blocks - 1, rows_j, rows), *[tiles(blocks, rows)] * 4,
             tiles(y_count, rows), tiles(y_count, rows),
             tiles(2, y_count, rows_j), tiles(z_count, rows), tiles(blocks, rows),
             pltpu.SemaphoreType.DMA((5,)), pltpu.SemaphoreType.DMA((EXCHANGES,)), pltpu.SemaphoreType.DMA((EXCHANGES,)),

time: 51.3 us -> 49 us (0.955)
  Pallas kernels: 50.6 us -> 48.2 us
    pallas_call x1, Pallas kernels: 49.9 us -> 47.6 us  [per_device(): pl.pallas_call(functools.partial(kernel, x_count, y_count, z_count), out_...]
where the time goes in v4:
time: 49 us; the launch traced here: 48.9 us
  Pallas kernels  48.2 us (98%)
  between operations  0.64 us (1%)
    pallas_call x1, Pallas kernels, per_device(): pl.pallas_call(functools.partial(kernel, x_count, y_count, z_count), out_...  47.6 us

profile of v4, /device:TPU:1, one launch (start us, length us, event | category | flops | bytes accessed | tf_op | source)
XLA Modules:
  0.0 48.9 jit_solution(411342868686427480)
XLA Ops:
  0.6 47.6 %shard_map.84 = (f32[128,128]{1,0:T(8,128)S(1)}, f32[8,128]{1,0:T(8,128)S(1)}, f32[128,128]{1,0:T(8,128)S(1)}, f32[1,128]{1,0:T(1,128)S(1)}) custom-call(f32[1024,128]{1,0:T(8,128)} %bitcast.5, f32[2,64,128]{2,1,0:T(8,128)} %bitcast.6, f32[8,128]{1,0:T(8,128)} %b_in.1, f32[8,16,128]{2,1,0:T(8,128)} %bitcast.7, f32[1,128]{1,0:T(1,128)} %bitcast.8), custom_call_target="tpu_custom_call" | custom-call | tf_op jit(solution)/shard_map/pallas_call | solution.py:373
  48.2 0.7 %shard_map.85 = (f32[128,128]{1,0:T(8,128)}, f32[8,128]{1,0:T(8,128)}, f32[128,128]{1,0:T(8,128)}, f32[1,128]{1,0:T(1,128)}) custom-call(f32[128,128]{1,0:T(8,128)S(1)} %get-tuple-element.12.refs_0_, f32[8,128]{1,0:T(8,128)S(1)} %get-tuple-element.13.refs_1_, f32[128,128]{1,0:T(8,128)S(1)} %get-tuple-element.14.refs_2_, f32[1,128]{1,0:T(1,128)S(1)} %get-tuple-element.15.refs_3_), custom_call_target="tpu_custom_call" | custom-call | tf_op jit(solution)/shard_map/pallas_call | solution.py:397

commit v5 on v4

--- a/solution.py
+++ b/solution.py
@@ -143,17 +143,24 @@
     c_right = right_operand(c)
     loads[2].wait()
     loads[0].wait()
-    total = jnp.zeros((rows_i, RANK), jnp.float32)
-    for j in range(rows_j):
-        product = dot_split(left_operand(e_v[pl.ds(j, rows_i, stride=rows_j), :]), c_right)
-        contracted[j] = product
-        total = total + product * b_v[j : j + 1, :]
-    part_a[...] = total.reshape(part_a.shape)
-    line_b[core, y] = b_v[...]
-
+    half = rows_i // 2
+
+    def voxel_terms(side):
+        start = pl.multiple_of(side * half, half)
+        total = jnp.zeros((half, RANK), jnp.float32)
+        for j in range(rows_j):
+            rows = e_v[pl.ds(start * rows_j + j, half, stride=rows_j), :]
+            product = dot_split(left_operand(rows), c_right)
+            contracted[j, pl.ds(start, half), :] = product
+            total = total + product * b_v[j : j + 1, :]
+        part_a[side] = total
+
+    voxel_terms(1 - core)
     pl.semaphore_wait(barrier, len(greeted))
     copy(part_a.at[1 - core], pair_a, PAIR_A, partner)
+    line_b[core, y] = b_v[...]
     gather_line(copy, line_b, core, y, y_count, y_peer, LINE_B)
+    voxel_terms(core)
     take(pair_a, PAIR_A)
     line_a[y] = part_a[core] + pair_a[...]
     gather(line_a, y, y_peer, LINE_A)
@@ -173,8 +180,11 @@
     b_left = left_operand(b_own)
 
     def turn(own, partners):
-        filler = jnp.zeros((RANK - 2 * rows_j, RANK), jnp.float32)
-        return jnp.concatenate([own, partners, filler], axis=0).T
+        first = lax.broadcasted_iota(jnp.int32, (8, RANK), 0) == 0
+        tiles = [
+            jnp.where(first, rows[n : n + 1], 0.0) for n in range(rows_j) for rows in (own, partners)
+        ]
+        return jnp.concatenate(tiles, axis=0).T
 
     take(line_b.at[0, pl.ds(0, y_count - 1)], LINE_B)
     copy(line_b.at[core], line_b.at[core], PAIR_B, partner)
@@ -202,8 +212,7 @@
     raw_terms = jnp.concatenate(
         [jnp.sum(contracted[j] * moved_a, axis=0, keepdims=True) for j in range(rows_j)], axis=0
     )
-    filler = jnp.zeros((RANK - rows_j, RANK), jnp.float32)
-    packed = pack(jnp.concatenate([raw_terms, filler], axis=0).T, strip, rows_j)
+    packed = pack(raw_terms, strip)
     for n in range(block_count):
         terms_part[n] = packed[n]
     for n, at in enumerate(block_peers):
@@ -214,7 +223,7 @@
     for j in range(rows_j):
         product = dot_split(a_left, e_right[j])
         strips[:, j] = product.reshape(block_count, strip, RANK)
-        fixed = fixed + product * b_turned[:, j : j + 1]
+        fixed = fixed + product * b_turned[:, j * strip : j * strip + 1]
     fixed_part[...] = fixed.reshape(fixed_part.shape)
     scatter(fixed_part, fixed_got, FIXED_SCATTER)
     for n, at in enumerate(block_peers):
@@ -239,14 +248,12 @@
     pull = dot_split(left_operand(w_gram_c_v[block] * gram_strip), b_turned_right)
     take(others(terms_z), TERMS_Z)
     terms = jnp.sum(terms_z[...], axis=0)
+    lanes = lax.broadcasted_iota(jnp.int32, (strip, RANK), 1)
+    strip_terms = jnp.where(lanes % strip == 0, spread(terms[0:1], strip, 0), spread(terms[1:2], strip, 8))
+    pull = pull - strip_terms * w_turned[block]
     terms_all[block, pl.ds(core, 1), :] = terms[0:1]
     terms_all[block, pl.ds(1 - core, 1), :] = terms[1:2]
     gather_blocks(terms_all, TERMS_GATHER)
-    lanes = lax.broadcasted_iota(jnp.int32, (strip, RANK), 1)
-    strip_terms = jnp.where(
-        lanes < rows_j, unpack(terms[0:1], strip, rows_j, 0), unpack(terms[1:2], strip, rows_j, rows_j)
-    )
-    pull = pull - strip_terms * w_turned[block]
     take(strips_got, STRIPS)
     total = None
     for j in range(rows_j):
@@ -254,16 +261,13 @@
         for n, (_, flip) in enumerate(block_peers):
             got = strips_got[n, j]
             by_core[flip] = got if by_core[flip] is None else by_core[flip] + got
-        term = by_core[0] * pull[:, j : j + 1] + by_core[1] * pull[:, rows_j + j : rows_j + j + 1]
+        term = by_core[0] * pull[:, j * strip : j * strip + 1] + by_core[1] * pull[:, j * strip + 8 : j * strip + 9]
         total = term if total is None else total + term
     step_line[y] = total
     gather(step_line, y, y_peer, LINE_STEP)
 
     take(others(terms_all), TERMS_GATHER)
-    columns = [
-        unpack(terms_all[n, pl.ds(core, 1), :], strip, rows_j, 0) for n in range(block_count)
-    ]
-    terms_b = jnp.concatenate(columns, axis=0).T[:rows_j] * w
+    terms_b = w * unpack([terms_all[n, pl.ds(core, 1), :] for n in range(block_count)], strip)
     take(others(gram_all), GRAM_GATHER)
     gram_a = whole(gram_all)
     coupled = w_gram_c * gram_a
@@ -330,21 +334,32 @@
     return value
 
 
-def pack(columns, strip, count):
+def chunks(strip):
+    return lax.broadcasted_iota(jnp.int32, (8, RANK), 0), lax.broadcasted_iota(jnp.int32, (8, RANK), 1) // strip
+
+
+def pack(samples, strip):
+    row, chunk = chunks(strip)
+    moved = slide(samples, 0, strip)
     rows = []
-    for start in range(0, RANK, strip):
-        row = None
-        for n in range(0, strip, 8):
-            tile = slide(columns[start + n : start + n + 8], n * count, count)
-            part = jnp.sum(tile, axis=0, keepdims=True)
-            row = part if row is None else row + part
-        rows.append(row)
+    for n in range(RANK // strip):
+        tile = pltpu.roll(moved, -n * strip % RANK, 1) if n else moved
+        rows.append(jnp.sum(jnp.where(chunk == row, tile, 0.0), axis=0, keepdims=True))
     return rows
 
 
-def unpack(row, strip, count, lane):
-    tile = jnp.broadcast_to(row, (8, RANK))
-    return jnp.concatenate([slide(tile, lane - n * count, -count) for n in range(0, strip, 8)], axis=0)
+def unpack(rows, strip):
+    row, chunk = chunks(strip)
+    total = jnp.zeros((8, RANK), jnp.float32)
+    for n, packed in enumerate(rows):
+        packed = pltpu.roll(packed, n * strip % RANK, 1) if n else packed
+        total = jnp.where(chunk == (row + n) % 8, jnp.broadcast_to(packed, (8, RANK)), total)
+    return slide(total, 0, -strip)
+
+
+def spread(packed, strip, lane):
+    tile = jnp.broadcast_to(packed, (8, RANK))
+    return jnp.concatenate([slide(tile, lane - n, -1) for n in range(0, strip, 8)], axis=0)
 
 
 def gather_line(copy, buffer, core, y, y_count, y_peer, exchange):

time: 49 us -> 48.9 us (level)
  no operation moved by 1% of the time
where the time goes in v5:
time: 48.9 us; the launch traced here: 48.8 us
  Pallas kernels  48.1 us (98%)
  between operations  0.64 us (1%)
    pallas_call x1, Pallas kernels, per_device(): pl.pallas_call(functools.partial(kernel, x_count, y_count, z_count), out_...  47.4 us

profile of v5, /device:TPU:1, one launch (start us, length us, event | category | flops | bytes accessed | tf_op | source)
XLA Modules:
  0.0 48.8 jit_solution(9790720933553923601)
XLA Ops:
  0.6 47.4 %shard_map.84 = (f32[128,128]{1,0:T(8,128)S(1)}, f32[8,128]{1,0:T(8,128)S(1)}, f32[128,128]{1,0:T(8,128)S(1)}, f32[1,128]{1,0:T(1,128)S(1)}) custom-call(f32[1024,128]{1,0:T(8,128)} %bitcast.5, f32[2,64,128]{2,1,0:T(8,128)} %bitcast.6, f32[8,128]{1,0:T(8,128)} %b_in.1, f32[8,16,128]{2,1,0:T(8,128)} %bitcast.7, f32[1,128]{1,0:T(1,128)} %bitcast.8), custom_call_target="tpu_custom_call" | custom-call | tf_op jit(solution)/shard_map/pallas_call | solution.py:388
  48.1 0.7 %shard_map.85 = (f32[128,128]{1,0:T(8,128)}, f32[8,128]{1,0:T(8,128)}, f32[128,128]{1,0:T(8,128)}, f32[1,128]{1,0:T(1,128)}) custom-call(f32[128,128]{1,0:T(8,128)S(1)} %get-tuple-element.12.refs_0_, f32[8,128]{1,0:T(8,128)S(1)} %get-tuple-element.13.refs_1_, f32[128,128]{1,0:T(8,128)S(1)} %get-tuple-element.14.refs_2_, f32[1,128]{1,0:T(1,128)S(1)} %get-tuple-element.15.refs_3_), custom_call_target="tpu_custom_call" | custom-call | tf_op jit(solution)/shard_map/pallas_call | solution.py:412
